TPU v7x, 32 devices: a whole 2x2x4 slice. The times are simulated.
32 devices in a mesh: fsdp: 8 (over z, y), seq: 4 (over x, core).
Axes of the slice: x: 2, y: 2, z: 4, core: 2. Of those that a mesh axis runs over, the one named last changes fastest.
Arguments:
- activations: bfloat16 [8, 2560, 1024], P('fsdp', 'seq'), may hold values from -6 to 6
- cotangent: bfloat16 [8, 2560, 1024], P('fsdp', 'seq'), may hold values from -6 to 6
- gain_attn: bfloat16 [1024], P('fsdp'), may hold values from 0.25 to 1.75
- w_qkv: bfloat16 [1024, 3072], P('fsdp'), may hold values from -0.25 to 0.25
- w_attn_out: bfloat16 [1024, 1024], P('fsdp'), may hold values from -0.75 to 0.75
- gain_mlp: bfloat16 [1024], P('fsdp'), may hold values from 0.25 to 1.75
- w_in: bfloat16 [1024, 5248], P('fsdp'), may hold values from -0.1875 to 0.1875
- w_mlp_out: bfloat16 [2624, 1024], P('fsdp'), may hold values from -0.125 to 0.125
Outputs:
- output: bfloat16 [8, 2560, 1024], P('fsdp', 'seq')
- d_input: bfloat16 [8, 2560, 1024], P('fsdp', 'seq')
- grad_gain_attn: float32 [1024], P('fsdp')
- grad_gain_mlp: float32 [1024], P('fsdp')
- grad_w_qkv: float32 [1024, 3072], P('fsdp')
- grad_w_attn_out: float32 [1024, 1024], P('fsdp')
- grad_w_in: float32 [1024, 5248], P('fsdp')
- grad_w_mlp_out: float32 [2624, 1024], P('fsdp')
All inputs are finite; a program needn't handle non-finite values.
Results may differ from a plain program's by a relative error of at most 0.023.
Values may be sent and summed in bfloat16 or wider, within the bound.
No kernel may reach another device: no remote copies, remote signals or barrier semaphores. Data moves between devices by JAX's collectives and lax.ppermute only.
A program may use at most 192 MiB of HBM per device.

v0:
```python
import math
import jax
import jax.numpy as jnp
from jax import lax
from jax.sharding import PartitionSpec as P

HEADS = 16
HEAD = 64
FF = 2624
LENGTH = 2560
QB = 512
eps = 1e-05
rope_base = 160000.0


def layer_norm(values, gain_vec):
    average = jnp.mean(values, -1, keepdims=True)
    centred = values - average
    variance = jnp.mean(centred * centred, -1, keepdims=True)
    return centred * lax.rsqrt(variance + eps) * gain_vec


def gelu_exact(values):
    return 0.5 * values * (1.0 + lax.erf(values * 2.0 ** (-0.5)))


def rope_tables(positions):
    half_size = HEAD // 2
    freq_index = jnp.arange(half_size).astype(positions.dtype)
    inverse = jnp.exp(freq_index * (-2.0 * math.log(rope_base) / HEAD))
    angles = positions[:, None] * inverse[None, :]
    angles = jnp.concatenate([angles, angles], 1)
    return (jnp.cos(angles), jnp.sin(angles))


def rotate(tensor, cosine, sine_table):
    half_size = HEAD // 2
    first = tensor[..., :half_size]
    second = tensor[..., half_size:]
    turned = jnp.concatenate([-second, first], -1)
    return tensor * cosine + turned * sine_table


def contract_rows(left, right):
    return lax.dot_general(
        left, right, (((0,), (0,)), ((), ())), preferred_element_type=jnp.float32
    )


def times_transpose(left, right):
    return lax.dot_general(
        left, right, (((1,), (1,)), ((), ())), preferred_element_type=jnp.float32
    )


def split_heads(packed_heads):
    local_heads = packed_heads.shape[2] // HEAD
    queries = packed_heads[:, 0].reshape(LENGTH // QB, QB, local_heads, HEAD)
    key_rows = packed_heads[:, 1].reshape(LENGTH, local_heads, HEAD)
    value_rows = packed_heads[:, 2].reshape(LENGTH, local_heads, HEAD)
    return (local_heads, queries, key_rows, value_rows)


def attend_sequence(packed_heads):
    local_heads, queries, key_rows, value_rows = split_heads(packed_heads)
    factor = float(HEAD) ** (-0.5)

    def one_block(q_block):
        scores = (
            jnp.einsum("qhd,khd->hqk", q_block, key_rows, preferred_element_type=jnp.float32)
            * factor
        )
        row_peak = jnp.max(scores, -1, keepdims=True)
        exponent = jnp.exp(scores - row_peak)
        row_total = jnp.sum(exponent, -1, keepdims=True)
        probs = (exponent / row_total).astype(jnp.bfloat16)
        attended = jnp.einsum("hqk,khd->qhd", probs, value_rows, preferred_element_type=jnp.float32)
        attended = attended.astype(jnp.bfloat16).reshape(QB, local_heads * HEAD)
        return (attended, (row_peak + jnp.log(row_total))[..., 0])

    attended, log_sums = lax.map(one_block, queries)
    return (attended.reshape(LENGTH, local_heads * HEAD), log_sums)


def attend_backward(pieces):
    packed_heads, log_sums, grad_heads = pieces
    local_heads, queries, key_rows, value_rows = split_heads(packed_heads)
    factor = float(HEAD) ** (-0.5)
    grad_blocks = grad_heads.reshape(LENGTH // QB, QB, local_heads, HEAD)

    def one_block(carry, block_pieces):
        key_grad, value_grad = carry
        q_block, lse_block, g_block = block_pieces
        scores = (
            jnp.einsum("qhd,khd->hqk", q_block, key_rows, preferred_element_type=jnp.float32)
            * factor
        )
        probs = jnp.exp(scores - lse_block[..., None])
        value_grad = value_grad + jnp.einsum(
            "hqk,qhd->khd", probs.astype(jnp.bfloat16), g_block, preferred_element_type=jnp.float32
        )
        prob_grad = jnp.einsum(
            "qhd,khd->hqk", g_block, value_rows, preferred_element_type=jnp.float32
        )
        inner = jnp.sum(probs * prob_grad, -1, keepdims=True)
        score_grad = (probs * (prob_grad - inner)).astype(jnp.bfloat16)
        query_grad = (
            jnp.einsum("hqk,khd->qhd", score_grad, key_rows, preferred_element_type=jnp.float32)
            * factor
        )
        key_grad = (
            key_grad
            + jnp.einsum("hqk,qhd->khd", score_grad, q_block, preferred_element_type=jnp.float32)
            * factor
        )
        return ((key_grad, value_grad), query_grad)

    zeros_state = jnp.zeros((LENGTH, local_heads, HEAD), jnp.float32)
    (key_grad, value_grad), query_grad = lax.scan(
        one_block, (zeros_state, zeros_state), (queries, log_sums, grad_blocks)
    )
    width_local = local_heads * HEAD
    stacked = jnp.stack(
        [
            query_grad.reshape(LENGTH, width_local),
            key_grad.reshape(LENGTH, width_local),
            value_grad.reshape(LENGTH, width_local),
        ],
        1,
    )
    return stacked.astype(jnp.bfloat16)


def local(activations, cotangent, gain_attn, w_qkv, w_attn_out, gain_mlp, w_in, w_mlp_out):
    local_seqs, positions, width = activations.shape
    row_count = local_seqs * positions
    gathered = (
        lax.all_gather(gain_attn, "fsdp", axis=0, tiled=True),
        lax.all_gather(w_qkv, "fsdp", axis=0, tiled=True),
        lax.all_gather(w_attn_out, "fsdp", axis=0, tiled=True),
        lax.all_gather(gain_mlp, "fsdp", axis=0, tiled=True),
        lax.all_gather(w_in, "fsdp", axis=0, tiled=True),
        lax.all_gather(w_mlp_out, "fsdp", axis=0, tiled=True),
    )
    full_gain_attn, full_qkv, full_attn_out, full_gain_mlp, full_in, full_mlp_out = gathered
    tokens = activations.astype(jnp.float32).reshape(row_count, width)
    normed, first_back = jax.vjp(layer_norm, tokens, full_gain_attn.astype(jnp.float32))
    normed_low = normed.astype(jnp.bfloat16)
    packed = jnp.dot(normed_low, full_qkv, preferred_element_type=jnp.float32)
    packed = packed.reshape(local_seqs, positions, 3, HEADS, HEAD)
    starting = (lax.axis_index("seq") * positions).astype(jnp.float32)
    places = starting + jnp.arange(positions).astype(jnp.float32)
    cosine, sine_table = rope_tables(places)

    def turn_pair(pair_values):
        return rotate(pair_values, cosine[:, None, None, :], sine_table[:, None, None, :])

    turned, turn_back = jax.vjp(turn_pair, packed[:, :, :2])
    rotated = jnp.concatenate([turned, packed[:, :, 2:]], 2).astype(jnp.bfloat16)
    rotated = rotated.reshape(local_seqs, positions, 3, width)
    heads_layout = lax.all_to_all(rotated, "seq", split_axis=3, concat_axis=1, tiled=True)
    attended_heads, log_sums = lax.map(attend_sequence, heads_layout)
    attended = lax.all_to_all(attended_heads, "seq", split_axis=1, concat_axis=2, tiled=True)
    attended_rows = attended.reshape(row_count, width)
    mixed = tokens + jnp.dot(attended_rows, full_attn_out, preferred_element_type=jnp.float32)
    normed_mlp, norm_back = jax.vjp(layer_norm, mixed, full_gain_mlp.astype(jnp.float32))
    normed_mlp_low = normed_mlp.astype(jnp.bfloat16)
    gate_up = jnp.dot(normed_mlp_low, full_in, preferred_element_type=jnp.float32)

    def gated(gate_part, up_part):
        return gelu_exact(gate_part) * up_part

    hidden, gated_back = jax.vjp(gated, gate_up[:, :FF], gate_up[:, FF:])
    hidden_low = hidden.astype(jnp.bfloat16)
    result = mixed + jnp.dot(hidden_low, full_mlp_out, preferred_element_type=jnp.float32)
    output = result.astype(jnp.bfloat16).reshape(activations.shape)
    again = (
        lax.all_gather(w_qkv, "fsdp", axis=0, tiled=True),
        lax.all_gather(w_attn_out, "fsdp", axis=0, tiled=True),
        lax.all_gather(w_in, "fsdp", axis=0, tiled=True),
        lax.all_gather(w_mlp_out, "fsdp", axis=0, tiled=True),
    )
    again_qkv, again_attn_out, again_in, again_mlp_out = again
    out_grad = cotangent.reshape(row_count, width)
    grad_mlp_out = contract_rows(hidden_low, out_grad)
    hidden_grad = times_transpose(out_grad, again_mlp_out)
    gate_grad, up_grad = gated_back(hidden_grad)
    gate_up_grad = jnp.concatenate([gate_grad, up_grad], 1).astype(jnp.bfloat16)
    grad_in = contract_rows(normed_mlp_low, gate_up_grad)
    normed_mlp_grad = times_transpose(gate_up_grad, again_in)
    mixed_grad_norm, grad_gain_mlp = norm_back(normed_mlp_grad)
    mixed_grad = out_grad.astype(jnp.float32) + mixed_grad_norm
    mixed_low = mixed_grad.astype(jnp.bfloat16)
    grad_attn_out = contract_rows(attended_rows, mixed_low)
    attended_grad = times_transpose(mixed_low, again_attn_out).astype(jnp.bfloat16)
    attended_grad = attended_grad.reshape(local_seqs, positions, width)
    grad_heads = lax.all_to_all(attended_grad, "seq", split_axis=2, concat_axis=1, tiled=True)
    rotated_grad = lax.map(attend_backward, (heads_layout, log_sums, grad_heads))
    position_grad = lax.all_to_all(rotated_grad, "seq", split_axis=1, concat_axis=3, tiled=True)
    position_grad = position_grad.astype(jnp.float32).reshape(local_seqs, positions, 3, HEADS, HEAD)
    (pair_grad,) = turn_back(position_grad[:, :, :2])
    packed_grad = jnp.concatenate([pair_grad, position_grad[:, :, 2:]], 2).astype(jnp.bfloat16)
    packed_grad = packed_grad.reshape(row_count, 3 * width)
    grad_qkv = contract_rows(normed_low, packed_grad)
    normed_grad = times_transpose(packed_grad, again_qkv)
    token_grad_norm, grad_gain_attn = first_back(normed_grad)
    d_input = (mixed_grad + token_grad_norm).astype(jnp.bfloat16).reshape(activations.shape)
    gradients = (grad_gain_attn, grad_gain_mlp, grad_qkv, grad_attn_out, grad_in, grad_mlp_out)
    shards = (
        lax.psum_scatter(
            gradients[0].astype(jnp.bfloat16), "fsdp", scatter_dimension=0, tiled=True
        ).astype(jnp.float32),
        lax.psum_scatter(
            gradients[1].astype(jnp.bfloat16), "fsdp", scatter_dimension=0, tiled=True
        ).astype(jnp.float32),
        lax.psum_scatter(
            gradients[2].astype(jnp.bfloat16), "fsdp", scatter_dimension=0, tiled=True
        ).astype(jnp.float32),
        lax.psum_scatter(
            gradients[3].astype(jnp.bfloat16), "fsdp", scatter_dimension=0, tiled=True
        ).astype(jnp.float32),
        lax.psum_scatter(
            gradients[4].astype(jnp.bfloat16), "fsdp", scatter_dimension=0, tiled=True
        ).astype(jnp.float32),
        lax.psum_scatter(
            gradients[5].astype(jnp.bfloat16), "fsdp", scatter_dimension=0, tiled=True
        ).astype(jnp.float32),
    )
    shards = (
        lax.psum(shards[0].astype(jnp.bfloat16), "seq").astype(jnp.float32),
        lax.psum(shards[1].astype(jnp.bfloat16), "seq").astype(jnp.float32),
        lax.psum(shards[2].astype(jnp.bfloat16), "seq").astype(jnp.float32),
        lax.psum(shards[3].astype(jnp.bfloat16), "seq").astype(jnp.float32),
        lax.psum(shards[4].astype(jnp.bfloat16), "seq").astype(jnp.float32),
        lax.psum(shards[5].astype(jnp.bfloat16), "seq").astype(jnp.float32),
    )
    return (output, d_input, shards[0], shards[1], shards[2], shards[3], shards[4], shards[5])


def solution(mesh):
    in_specs = (
        P("fsdp", "seq", None),
        P("fsdp", "seq", None),
        P("fsdp"),
        P("fsdp", None),
        P("fsdp", None),
        P("fsdp"),
        P("fsdp", None),
        P("fsdp", None),
    )
    out_specs = (
        P("fsdp", "seq", None),
        P("fsdp", "seq", None),
        P("fsdp"),
        P("fsdp"),
        P("fsdp", None),
        P("fsdp", None),
        P("fsdp", None),
        P("fsdp", None),
    )
    return jax.shard_map(local, mesh=mesh, in_specs=in_specs, out_specs=out_specs, check_vma=False)
```

profile of v0, /device:TPU:0, one launch (start us, length us, event | category | flops | bytes accessed | tf_op | source)
XLA Modules:
  0.0 1313.2 jit_solution(7243004674187600519)
XLA Ops:
  9.4 22.5 %all-gather = bf16[8,1,128]{2,1,0:T(2,128)(2,1)S(1)} all-gather(bf16[1,1,128]{2,1,0:T(2,128)(2,1)} %bitcast.228), channel_id=1, replica_groups=mesh['fsdp'=8,'seq'=4] {'fsdp'}, dimensions={0}, use_global_device_ids=true | all-gather | bytes 2304 | tf_op jit(solution)/shard_map/all_gather | solution.py:138
  33.7 78.3 %all-gather.7.cloned.1.call-done = bf16[1024,3072]{1,0:T(8,128)(2,1)} async-done(((bf16[128,3072]{1,0:T(8,128)(2,1)}), bf16[1024,3072]{1,0:T(8,128)(2,1)}) %all-gather.7.cloned.1.call-update) | async-done | bytes 6291472 | tf_op jit(solution)/shard_map/all_gather | solution.py:139
  147.1 58.9 %all-to-all-done = bf16[1,640,3,1024]{1,2,0,3:T(4,128)(2,1)} async-done(((bf16[1,640,3,1024]{1,2,0,3:T(4,128)(2,1)}), bf16[1,640,3,1024]{1,2,0,3:T(4,128)(2,1)}, u32[]{:S(2)}, u32[]{:S(2)}) %all-to-all-start) | async-done | bytes 3932192 | tf_op jit(solution)/shard_map/all_to_all | solution.py:161
  228.4 93.1 %while.45 = (s32[]{:T(128)}, bf16[5,512,256]{2,1,0:T(8,128)(2,1)}, f32[5,4,512]{2,1,0:T(4,128)}, bf16[5,512,4,64]{1,3,2,0:T(8,128)(2,1)}, bf16[2560,4,64]{0,2,1:...) while((s32[]{:T(128)}, bf16[5,512,256]{2,1,0:T(8,128)(2,1)}, f32[5,4,512]{2,1,0:T(4,128)}, ...), condition=%wide.region_5.0_spmd, body=%wide.region_2.5_spmd.sunk | while | flops 1389492224 | bytes 67174496 | solution.py:81
  347.5 17.7 %all-gather.1 = bf16[8,1,128]{2,1,0:T(2,128)(2,1)S(1)} all-gather(bf16[1,1,128]{2,1,0:T(2,128)(2,1)S(1)} %bitcast.229), channel_id=1, replica_groups=mesh['fsdp'=8,'seq'=4] {'fsdp'}, dimensions={0}, use_global_device_ids=true | all-gather | bytes 2304 | tf_op jit(solution)/shard_map/all_gather | solution.py:141
  377.1 15.1 %fusion.73 = f32[640,5248]{1,0:T(8,128)} fusion(bf16[1024,5248]{1,0:T(8,128)(2,1)} %all-gather.11.cloned.1.call-done, f32[640,1024]{1,0:T(8,128)} %copy-done.7, f32[1024]{0:T(1024)S(1)} %bitcast.224, f32[640]{0:T(1024)S(1)} %fusion.67, f32[640]{0:T(1024)S(1)} %broadcast_multiply_fusion.1), kind=kOutput, calls=%fused_computation.125 | convolution fusion | flops 6881280000 | bytes 26813440 | tf_op jit(solution)/shard_map/dot_general | solution.py:168
  404.5 14.9 %add_convert_fusion = (bf16[640,2624]{1,0:T(8,128)(2,1)S(1)}, bf16[640,2624]{1,0:T(8,128)(2,1)}, bf16[640,2624]{1,0:T(8,128)(2,1)}) fusion(f32[640,5248]{1,0:T(8,128)} %fusion.73, bf16[2624,1024]{1,0:T(8,128)(2,1)} %all-gather.13.cloned.1.call-done, bf16[1,640,1024]{2,1,0:T(8,128)(2,1)} %param.13), kind=kOutput, calls=%fused_computation.48 | convolution fusion | flops 3471237120 | bytes 30195712 | tf_op jit(solution)/shard_map/dot_general | solution.py:51
  419.4 14.6 %multiply_reduce_fusion.2 = (bf16[1024]{0:T(1024)(128)(2,1)}, f32[640]{0:T(1024)S(1)}, f32[640,1024]{1,0:T(8,128)S(1)}) fusion(f32[640,1024]{1,0:T(8,128)S(1)} %copy-done.8, f32[640]{0:T(1024)S(1)} %fusion.67, f32[640]{0:T(1024)S(1)} %broadcast_multiply_fusion.1, f32[1024]{0:T(1024)S(1)} %bitcast.225, bf16[1024,5248]{1,0:T(8,128)(2,1)} %all-gather.11.cloned.1.call-done, ...), kind=kOutput, calls=%fused_computation.88 | convolution fusion | flops 6896679424 | bytes 22722048 | tf_op jit(solution)/shard_map/dot_general | solution.py:51
  490.0 323.5 %while.46 = (s32[]{:T(128)}, f32[2560,4,64]{0,2,1:T(8,128)}, f32[2560,4,64]{0,2,1:T(8,128)}, bf16[5,512,4,64]{1,3,2,0:T(8,128)(2,1)}, bf16[5,512,4,64]{1,3,2,0:T...) while((s32[]{:T(128)}, f32[2560,4,64]{0,2,1:T(8,128)}, ...), condition=%wide.region_12.13_spmd.clone, body=%wide.region_10.12_spmd.clone.sunk | while | flops 3421763584 | bytes 173334672 | solution.py:119
  514.8 14.7 %multiply_reduce_fusion.8 = (f32[4,512]{1,0:T(4,128)S(1)}, f32[4,512,2560]{2,1,0:T(8,128)}) fusion(f32[4,512,2560]{2,1,0:T(8,128)} %fusion.130, f32[4,512]{1,0:T(4,128)S(1)} %dynamic-slice_bitcast_fusion.2, bf16[2560,4,64]{0,2,1:T(8,128)(2,1)} %get-tuple-element.413, bf16[5,512,4,64]{1,3,2,0:T(8,128)(2,1)} %get-tuple-element.412, s32[]{:T(128)S(6)} %copy.94), kind=kOutput, calls=%fused_computation.14.clone.1 | convolution fusion | flops 692058112 | bytes 43532292 | tf_op jit(solution)/shard_map/while/body/eval_jaxpr/while/body/eval_jaxpr/qhd,khd->hqk/dot_general | solution.py:102
  529.5 15.1 %multiply_convert_fusion.7 = bf16[4,512,2560]{2,1,0:T(8,128)(2,1)S(1)} fusion(f32[4,512,2560]{2,1,0:T(8,128)} %get-tuple-element.360, f32[4,512,2560]{2,1,0:T(8,128)} %fusion.130, f32[4,512]{1,0:T(4,128)S(1)} %get-tuple-element.361, f32[4,512]{1,0:T(4,128)S(1)} %dynamic-slice_bitcast_fusion.2), kind=kLoop, calls=%fused_computation.13.clone.1 | loop fusion | flops 26214400 | bytes 52445184 | tf_op jit(solution)/shard_map/while/body/eval_jaxpr/while/body/eval_jaxpr/convert_element_type | solution.py:106
  580.2 14.3 %multiply_reduce_fusion.8 = (f32[4,512]{1,0:T(4,128)S(1)}, f32[4,512,2560]{2,1,0:T(8,128)}) fusion(f32[4,512,2560]{2,1,0:T(8,128)} %fusion.130, f32[4,512]{1,0:T(4,128)S(1)} %dynamic-slice_bitcast_fusion.2, bf16[2560,4,64]{0,2,1:T(8,128)(2,1)} %get-tuple-element.413, bf16[5,512,4,64]{1,3,2,0:T(8,128)(2,1)} %get-tuple-element.412, s32[]{:T(128)S(6)} %copy.94), kind=kOutput, calls=%fused_computation.14.clone.1 | convolution fusion | flops 692058112 | bytes 43532292 | tf_op jit(solution)/shard_map/while/body/eval_jaxpr/while/body/eval_jaxpr/qhd,khd->hqk/dot_general | solution.py:102
  594.4 14.7 %multiply_convert_fusion.7 = bf16[4,512,2560]{2,1,0:T(8,128)(2,1)S(1)} fusion(f32[4,512,2560]{2,1,0:T(8,128)} %get-tuple-element.360, f32[4,512,2560]{2,1,0:T(8,128)} %fusion.130, f32[4,512]{1,0:T(4,128)S(1)} %get-tuple-element.361, f32[4,512]{1,0:T(4,128)S(1)} %dynamic-slice_bitcast_fusion.2), kind=kLoop, calls=%fused_computation.13.clone.1 | loop fusion | flops 26214400 | bytes 52445184 | tf_op jit(solution)/shard_map/while/body/eval_jaxpr/while/body/eval_jaxpr/convert_element_type | solution.py:106
  645.1 14.2 %multiply_reduce_fusion.8 = (f32[4,512]{1,0:T(4,128)S(1)}, f32[4,512,2560]{2,1,0:T(8,128)}) fusion(f32[4,512,2560]{2,1,0:T(8,128)} %fusion.130, f32[4,512]{1,0:T(4,128)S(1)} %dynamic-slice_bitcast_fusion.2, bf16[2560,4,64]{0,2,1:T(8,128)(2,1)} %get-tuple-element.413, bf16[5,512,4,64]{1,3,2,0:T(8,128)(2,1)} %get-tuple-element.412, s32[]{:T(128)S(6)} %copy.94), kind=kOutput, calls=%fused_computation.14.clone.1 | convolution fusion | flops 692058112 | bytes 43532292 | tf_op jit(solution)/shard_map/while/body/eval_jaxpr/while/body/eval_jaxpr/qhd,khd->hqk/dot_general | solution.py:102
  659.3 14.3 %multiply_convert_fusion.7 = bf16[4,512,2560]{2,1,0:T(8,128)(2,1)S(1)} fusion(f32[4,512,2560]{2,1,0:T(8,128)} %get-tuple-element.360, f32[4,512,2560]{2,1,0:T(8,128)} %fusion.130, f32[4,512]{1,0:T(4,128)S(1)} %get-tuple-element.361, f32[4,512]{1,0:T(4,128)S(1)} %dynamic-slice_bitcast_fusion.2), kind=kLoop, calls=%fused_computation.13.clone.1 | loop fusion | flops 26214400 | bytes 52445184 | tf_op jit(solution)/shard_map/while/body/eval_jaxpr/while/body/eval_jaxpr/convert_element_type | solution.py:106
  723.8 14.3 %multiply_convert_fusion.7 = bf16[4,512,2560]{2,1,0:T(8,128)(2,1)S(1)} fusion(f32[4,512,2560]{2,1,0:T(8,128)} %get-tuple-element.360, f32[4,512,2560]{2,1,0:T(8,128)} %fusion.130, f32[4,512]{1,0:T(4,128)S(1)} %get-tuple-element.361, f32[4,512]{1,0:T(4,128)S(1)} %dynamic-slice_bitcast_fusion.2), kind=kLoop, calls=%fused_computation.13.clone.1 | loop fusion | flops 26214400 | bytes 52445184 | tf_op jit(solution)/shard_map/while/body/eval_jaxpr/while/body/eval_jaxpr/convert_element_type | solution.py:106
  774.1 14.2 %multiply_reduce_fusion.8 = (f32[4,512]{1,0:T(4,128)S(1)}, f32[4,512,2560]{2,1,0:T(8,128)}) fusion(f32[4,512,2560]{2,1,0:T(8,128)} %fusion.130, f32[4,512]{1,0:T(4,128)S(1)} %dynamic-slice_bitcast_fusion.2, bf16[2560,4,64]{0,2,1:T(8,128)(2,1)} %get-tuple-element.413, bf16[5,512,4,64]{1,3,2,0:T(8,128)(2,1)} %get-tuple-element.412, s32[]{:T(128)S(6)} %copy.94), kind=kOutput, calls=%fused_computation.14.clone.1 | convolution fusion | flops 692058112 | bytes 43532292 | tf_op jit(solution)/shard_map/while/body/eval_jaxpr/while/body/eval_jaxpr/qhd,khd->hqk/dot_general | solution.py:102
  788.3 14.3 %multiply_convert_fusion.7 = bf16[4,512,2560]{2,1,0:T(8,128)(2,1)S(1)} fusion(f32[4,512,2560]{2,1,0:T(8,128)} %get-tuple-element.360, f32[4,512,2560]{2,1,0:T(8,128)} %fusion.130, f32[4,512]{1,0:T(4,128)S(1)} %get-tuple-element.361, f32[4,512]{1,0:T(4,128)S(1)} %dynamic-slice_bitcast_fusion.2), kind=kLoop, calls=%fused_computation.13.clone.1 | loop fusion | flops 26214400 | bytes 52445184 | tf_op jit(solution)/shard_map/while/body/eval_jaxpr/while/body/eval_jaxpr/convert_element_type | solution.py:106
  834.2 63.3 %all_to_all.54 = bf16[1,2560,3,256]{3,2,0,1:T(4,128)(2,1)S(1)} all-to-all(bf16[1,2560,3,256]{3,2,0,1:T(4,128)(2,1)} %copy.65), channel_id=1, replica_groups=mesh['fsdp'=8,'seq'=4] {'seq'}, dimensions={1} | all-to-all | bytes 7864320 | tf_op jit(solution)/shard_map/all_to_all | solution.py:199
  929.3 15.7 %convolution_convert_fusion = bf16[1024,5248]{1,0:T(8,128)(2,1)} fusion(bf16[640,2624]{1,0:T(8,128)(2,1)} %get-tuple-element.246, bf16[640,2624]{1,0:T(8,128)(2,1)} %copy-done.41, f32[640,1024]{1,0:T(8,128)} %copy-done.7, f32[1024]{0:T(1024)S(1)} %bitcast.227, f32[640]{0:T(1024)S(1)} %copy-done.36, f32[640]{0:T(1024)S(1)} %copy-done.24), kind=kOutput, calls=%fused_computation.44 | convolution fusion | flops 6900088832 | bytes 20096000 | tf_op jit(solution)/shard_map/dot_general | solution.py:45
  956.3 88.0 %reduce-scatter.5.cloned.1.call-done = bf16[128,3072]{1,0:T(8,128)(2,1)} async-done(((bf16[1024,3072]{1,0:T(8,128)(2,1)}), bf16[128,3072]{1,0:T(8,128)(2,1)}) %reduce-scatter.5.cloned.1.call-update) | async-done | bytes 786448 | tf_op jit(solution)/shard_map/reduce_scatter | solution.py:216
  1044.3 185.0 %reduce-scatter.9.cloned.1.call-done = bf16[128,5248]{1,0:T(8,128)(2,1)} async-done(((bf16[1024,5248]{1,0:T(8,128)(2,1)}), bf16[128,5248]{1,0:T(8,128)(2,1)}) %reduce-scatter.9.cloned.1.call-update) | async-done | bytes 1343504 | tf_op jit(solution)/shard_map/reduce_scatter | solution.py:222
  1238.9 19.6 %all-reduce.4 = (bf16[1024]{0:T(1024)(128)(2,1)S(1)}, bf16[1024]{0:T(1024)(128)(2,1)S(1)}) all-reduce(bf16[1024]{0:T(1024)(128)(2,1)S(1)} %get-tuple-element.199, bf16[1024]{0:T(1024)(128)(2,1)S(1)} %copy-done.37), channel_id=2, replica_groups=mesh['fsdp'=8,'seq'=4] {'fsdp'}, use_global_device_ids=true, to_apply=%region_16.17.clone | all-reduce | flops 2048 | bytes 8192
  1269.7 29.3 %all-reduce.9.cloned.1.call-done = (bf16[128,3072]{1,0:T(8,128)(2,1)}, bf16[128,1024]{1,0:T(8,128)(2,1)}, bf16[128,5248]{1,0:T(8,128)(2,1)}, bf16[328,1024]{1,0:T(8,128)(2,1)}) async-done(((bf16[128,3072]{1,0:T(8,128)(2,1)}, bf16[128,1024]{1,0:T(8,128)(2,1)}, bf16[128,5248]{1,0:T(8,128)(2,1)}, bf16[328,1024]{1,0:T(8,128)(2,1)}), (bf16[128,3072]{1,0:T(8,128)(2,1)}, bf16[128,1024]{1,0:T(8,128)(2,1)}, ...) | async-done | bytes 3063824 | tf_op jit(solution)/shard_map/psum | solution.py:232
  (258 shorter events, 544.2 us)
Async XLA Ops:
  7.2 25.2 %copy-start.3 = (bf16[1,640,1024]{2,1,0:T(8,128)(2,1)S(1)}, bf16[1,640,1024]{2,1,0:T(8,128)(2,1)}, u32[]{:S(2)}) copy-start(bf16[1,640,1024]{2,1,0:T(8,128)(2,1)} %param.12) | copy-start | bytes 3932164
  7.2 104.8 %all-gather.7.cloned.1.call-start = ((), (), s32[]{:S(2)}) async-start(), calls=%async_computation.8 | async-start | bytes 7077888 | tf_op jit(solution)/shard_map/all_gather | solution.py:139
  7.9 363.6 %all-gather.9.cloned.1.call-start = ((), (), s32[]{:S(2)}) async-start(), calls=%async_computation.9 | async-start | bytes 2359296 | tf_op jit(solution)/shard_map/all_gather | solution.py:140
  8.7 368.4 %all-gather.11.cloned.1.call-start = ((), (), s32[]{:S(2)}) async-start(), calls=%async_computation.10 | async-start | bytes 12091392 | tf_op jit(solution)/shard_map/all_gather | solution.py:142
  31.9 88.7 %copy-start.27 = (f32[8,1,128]{2,1,0:T(1,128)}, f32[8,1,128]{2,1,0:T(1,128)S(1)}, u32[]{:S(2)}) copy-start(f32[8,1,128]{2,1,0:T(1,128)S(1)} %convert_element_type.213) | copy-start | bytes 12292
  32.3 98.8 %copy-start.14 = (f32[640,64]{0,1:T(8,128)}, f32[640,64]{0,1:T(8,128)S(1)}, u32[]{:S(2)}) copy-start(f32[640,64]{0,1:T(8,128)S(1)} %get-tuple-element.255) | copy-start | bytes 491524
  32.4 98.8 %copy-start.16 = (f32[640,64]{0,1:T(8,128)}, f32[640,64]{0,1:T(8,128)S(1)}, u32[]{:S(2)}) copy-start(f32[640,64]{0,1:T(8,128)S(1)} %get-tuple-element.256) | copy-start | bytes 491524
  32.6 88.0 %copy-start.21 = (f32[640]{0:T(1024)}, f32[640]{0:T(1024)S(1)}, u32[]{:S(2)}) copy-start(f32[640]{0:T(1024)S(1)} %broadcast_multiply_fusion.2) | copy-start | bytes 7684
  33.7 87.0 %copy-start.29 = (f32[640]{0:T(1024)}, f32[640]{0:T(1024)S(1)}, u32[]{:S(2)}) copy-start(f32[640]{0:T(1024)S(1)} %fusion.66) | copy-start | bytes 7684
  141.4 64.5 %all-to-all-start = ((bf16[1,640,3,1024]{1,2,0,3:T(4,128)(2,1)}), bf16[1,640,3,1024]{1,2,0,3:T(4,128)(2,1)}, u32[]{:S(2)}, u32[]{:S(2)}) async-start(bf16[1,640,3,1024]{1,2,0,3:T(4,128)(2,1)} %pad_maximum_fusion.1), calls=%async_computation | async-start | bytes 10485760 | tf_op jit(solution)/shard_map/all_to_all | solution.py:161
  146.5 258.0 %all-gather.13.cloned.1.call-start = ((), (), s32[]{:S(2)}) async-start(), calls=%async_computation.11 | async-start | bytes 6045696 | tf_op jit(solution)/shard_map/all_gather | solution.py:143
  343.9 21.3 %all-to-all-start.1 = ((bf16[4,2,81920]{2,1,0:T(2,128)(2,1)}), bf16[4,2,81920]{2,1,0:T(2,128)(2,1)S(1)}, u32[]{:S(2)}, u32[]{:S(2)}) async-start(bf16[4,2,81920]{2,1,0:T(2,128)(2,1)} %reshape.443), calls=%async_computation.1 | async-start | bytes 2621440 | tf_op jit(solution)/shard_map/all_to_all | solution.py:163
  347.5 608.8 %reduce-scatter.7.cloned.1.call-start = ((), (), s32[]{:S(2)}) async-start(), calls=%async_computation.13 | async-start | bytes 2359296 | tf_op jit(solution)/shard_map/reduce_scatter | solution.py:219
  365.2 68.8 %copy-start.33 = (f32[8,1,128]{2,1,0:T(1,128)}, f32[8,1,128]{2,1,0:T(1,128)S(1)}, u32[]{:S(2)}) copy-start(f32[8,1,128]{2,1,0:T(1,128)S(1)} %convert_element_type.214) | copy-start | bytes 12292
  375.2 58.9 %copy-start.23 = (f32[640]{0:T(1024)}, f32[640]{0:T(1024)S(1)}, u32[]{:S(2)}) copy-start(f32[640]{0:T(1024)S(1)} %broadcast_multiply_fusion.1) | copy-start | bytes 7684
  377.0 57.1 %copy-start.35 = (f32[640]{0:T(1024)}, f32[640]{0:T(1024)S(1)}, u32[]{:S(2)}) copy-start(f32[640]{0:T(1024)S(1)} %fusion.67) | copy-start | bytes 7684
  392.1 27.3 %copy-start.8 = (f32[640,1024]{1,0:T(8,128)S(1)}, f32[640,1024]{1,0:T(8,128)}, u32[]{:S(2)}) copy-start(f32[640,1024]{1,0:T(8,128)} %copy-done.7) | copy-start | bytes 7864324
  461.8 21.6 %all-to-all-start.2 = ((bf16[4,2,81920]{2,1,0:T(2,128)(2,1)}), bf16[4,2,81920]{2,1,0:T(2,128)(2,1)}, u32[]{:S(2)}, u32[]{:S(2)}) async-start(bf16[4,2,81920]{2,1,0:T(2,128)(2,1)} %reshape.445), calls=%async_computation.2 | async-start | bytes 2621440 | tf_op jit(solution)/shard_map/all_to_all | solution.py:197
  466.2 490.1 %reduce-scatter.11.cloned.1.call-start = ((), (), s32[]{:S(2)}) async-start(), calls=%async_computation.15 | async-start | bytes 6045696 | tf_op jit(solution)/shard_map/reduce_scatter | solution.py:225
  474.5 569.8 %reduce-scatter.5.cloned.1.call-start = ((), (), s32[]{:S(2)}) async-start(), calls=%async_computation.12 | async-start | bytes 7077888 | tf_op jit(solution)/shard_map/reduce_scatter | solution.py:216
  928.7 300.6 %reduce-scatter.9.cloned.1.call-start = ((), (), s32[]{:S(2)}) async-start(), calls=%async_computation.14 | async-start | bytes 12091392 | tf_op jit(solution)/shard_map/reduce_scatter | solution.py:222
  945.0 353.9 %all-reduce.9.cloned.1.call-start = ((), (), s32[]{:S(2)}) async-start(), calls=%async_computation.16 | async-start | bytes 6127616 | tf_op jit(solution)/shard_map/psum | solution.py:232
  1237.5 28.3 %copy-start.2 = (f32[640,1024]{1,0:T(8,128)S(1)}, f32[640,1024]{1,0:T(8,128)}, u32[]{:S(2)}) copy-start(f32[640,1024]{1,0:T(8,128)} %copy-done.1) | copy-start | bytes 7864324
  1237.5 28.2 %copy-start.32 = (f32[640]{0:T(1024)S(1)}, f32[640]{0:T(1024)}, u32[]{:S(2)}) copy-start(f32[640]{0:T(1024)} %copy-done.31) | copy-start | bytes 7684
  (32 other events, 110.6 us)
Sparse Core Ops, SparseCore 0:
  10.2 101.7 all-gather.6
  114.1 47.4 all-gather.8
  163.8 152.5 all-gather.10
  318.4 86.0 all-gather.12
  440.6 66.1 reduce-scatter.6
  510.2 103.5 reduce-scatter.10
  928.8 115.4 reduce-scatter.4
  1048.3 180.8 reduce-scatter.8
  1231.9 67.0 all-reduce.8
where the time goes:
time: 1320 us; the launch traced here: 1310 us
  waiting for transfers between devices  463 us (35%)
  matrix products  413 us (31%)
  other arithmetic  163 us (12%)
  blocking collectives  129 us (10%)
  local copies, waits for them, and re-layouts  116 us (9%)
  between operations  15.6 us (1%)
  starting transfers between devices  13.6 us (1%)
    reduce_scatter x1, waiting for transfers between devices, local(): lax.psum_scatter(gradients[4].astype(jnp.bfloat16), 'fsdp', scatter_dimen...  185 us
    reduce_scatter x1, waiting for transfers between devices, local(): lax.psum_scatter(gradients[2].astype(jnp.bfloat16), 'fsdp', scatter_dimen...  88 us
    dot_general x10, matrix products, one_block(): jnp.einsum('qhd,khd->hqk', q_block, key_rows, preferred_element_type=jnp....  79 us
    all_gather x1, waiting for transfers between devices, local(): lax.all_gather(w_qkv, 'fsdp', axis=0, tiled=True)  78.3 us
    convert_element_type x5, other arithmetic, one_block(): score_grad = (probs * (prob_grad - inner)).astype(jnp.bfloat16)  72.9 us
    dot_general x5, matrix products, one_block(): jnp.einsum('qhd,khd->hqk', g_block, value_rows, preferred_element_type=jn...  71.4 us
    dot_general x5, matrix products, one_block(): jnp.einsum('hqk,qhd->khd', probs.astype(jnp.bfloat16), g_block, preferred...  66 us
    all_to_all x1, blocking collectives, local(): lax.all_to_all(rotated_grad, 'seq', split_axis=1, concat_axis=3, tiled=True)  63.3 us
  transfers between devices with their start and end apart: 12, of which 7 were waited for; matrix products, arithmetic and copies ran while one was open for 49% of the time, Pallas kernels for 0%

commit v1 on v0

--- a/solution.py
+++ b/solution.py
@@ -229,7 +229,7 @@
     shards = (
         lax.psum(shards[0].astype(jnp.bfloat16), "seq").astype(jnp.float32),
         lax.psum(shards[1].astype(jnp.bfloat16), "seq").astype(jnp.float32),
-        lax.psum(shards[2].astype(jnp.bfloat16), "seq").astype(jnp.float32),
+        jnp.sum(lax.all_gather(shards[2].astype(jnp.bfloat16), "seq"), axis=0).astype(jnp.float32),
         lax.psum(shards[3].astype(jnp.bfloat16), "seq").astype(jnp.float32),
         lax.psum(shards[4].astype(jnp.bfloat16), "seq").astype(jnp.float32),
         lax.psum(shards[5].astype(jnp.bfloat16), "seq").astype(jnp.float32),

time: 1320 us -> 1510 us (1.14)
  waiting for transfers between devices: 463 us -> 636 us
    reduce_scatter x1, waiting for transfers between devices: 0.01 us -> 107 us  [local(): lax.psum_scatter(gradients[5].astype(jnp.bfloat16), 'fsdp', scatter_dimen...]
    reduce_scatter x1, waiting for transfers between devices: 0.01 us -> 50.4 us  [local(): lax.psum_scatter(gradients[3].astype(jnp.bfloat16), 'fsdp', scatter_dimen...]
    psum x1, waiting for transfers between devices: 29.3 us -> 48.7 us  [local(): lax.psum(shards[3].astype(jnp.bfloat16), 'seq').astype(jnp.float32)]
  transfers between devices with their start and end apart: 12 -> 13, of which waited for: 7 -> 9; matrix products, arithmetic and copies ran while one was open for 49% -> 17% of each run, Pallas kernels for 0% -> 0%
where the time goes in v1:
time: 1510 us; the launch traced here: 1500 us
  waiting for transfers between devices  636 us (42%)
  matrix products  415 us (27%)
  other arithmetic  166 us (11%)
  blocking collectives  129 us (9%)
  local copies, waits for them, and re-layouts  115 us (8%)
  starting transfers between devices  24.6 us (2%)
  between operations  15.7 us (1%)
    reduce_scatter x1, waiting for transfers between devices, local(): lax.psum_scatter(gradients[4].astype(jnp.bfloat16), 'fsdp', scatter_dimen...  185 us
    reduce_scatter x1, waiting for transfers between devices, local(): lax.psum_scatter(gradients[5].astype(jnp.bfloat16), 'fsdp', scatter_dimen...  107 us
    reduce_scatter x1, waiting for transfers between devices, local(): lax.psum_scatter(gradients[2].astype(jnp.bfloat16), 'fsdp', scatter_dimen...  85.7 us
    dot_general x10, matrix products, one_block(): jnp.einsum('qhd,khd->hqk', q_block, key_rows, preferred_element_type=jnp....  78.7 us
    all_gather x1, waiting for transfers between devices, local(): lax.all_gather(w_qkv, 'fsdp', axis=0, tiled=True)  78.3 us
    convert_element_type x5, other arithmetic, one_block(): score_grad = (probs * (prob_grad - inner)).astype(jnp.bfloat16)  71.7 us
    dot_general x5, matrix products, one_block(): jnp.einsum('qhd,khd->hqk', g_block, value_rows, preferred_element_type=jn...  71.6 us
    dot_general x5, matrix products, one_block(): jnp.einsum('hqk,qhd->khd', probs.astype(jnp.bfloat16), g_block, preferred...  65.3 us
  transfers between devices with their start and end apart: 13, of which 9 were waited for; matrix products, arithmetic and copies ran while one was open for 17% of the time, Pallas kernels for 0%

profile of v1, /device:TPU:0, one launch (start us, length us, event | category | flops | bytes accessed | tf_op | source)
XLA Modules:
  0.0 1502.1 jit_solution(16571441463862156562)
XLA Ops:
  9.4 22.5 %all-gather.1 = bf16[8,1,128]{2,1,0:T(2,128)(2,1)S(1)} all-gather(bf16[1,1,128]{2,1,0:T(2,128)(2,1)} %bitcast.230), channel_id=1, replica_groups=mesh['fsdp'=8,'seq'=4] {'fsdp'}, dimensions={0}, use_global_device_ids=true | all-gather | bytes 2304 | tf_op jit(solution)/shard_map/all_gather | solution.py:138
  33.7 78.3 %all-gather.9.cloned.1.call-done = bf16[1024,3072]{1,0:T(8,128)(2,1)} async-done(((bf16[128,3072]{1,0:T(8,128)(2,1)}), bf16[1024,3072]{1,0:T(8,128)(2,1)}) %all-gather.9.cloned.1.call-update) | async-done | bytes 6291472 | tf_op jit(solution)/shard_map/all_gather | solution.py:139
  157.7 48.3 %all-to-all-done = bf16[1,640,3,1024]{1,2,0,3:T(4,128)(2,1)} async-done(((bf16[1,640,3,1024]{1,2,0,3:T(4,128)(2,1)}), bf16[1,640,3,1024]{1,2,0,3:T(4,128)(2,1)}, u32[]{:S(2)}, u32[]{:S(2)}) %all-to-all-start) | async-done | bytes 3932192 | tf_op jit(solution)/shard_map/all_to_all | solution.py:161
  228.4 93.1 %while.45 = (s32[]{:T(128)}, bf16[5,512,256]{2,1,0:T(8,128)(2,1)}, f32[5,4,512]{2,1,0:T(4,128)}, bf16[5,512,4,64]{1,3,2,0:T(8,128)(2,1)}, bf16[2560,4,64]{0,2,1:...) while((s32[]{:T(128)}, bf16[5,512,256]{2,1,0:T(8,128)(2,1)}, f32[5,4,512]{2,1,0:T(4,128)}, ...), condition=%wide.region_5.0_spmd, body=%wide.region_2.5_spmd.sunk | while | flops 1389492224 | bytes 67174496 | solution.py:81
  347.5 17.7 %all-gather.2 = bf16[8,1,128]{2,1,0:T(2,128)(2,1)S(1)} all-gather(bf16[1,1,128]{2,1,0:T(2,128)(2,1)S(1)} %bitcast.231), channel_id=1, replica_groups=mesh['fsdp'=8,'seq'=4] {'fsdp'}, dimensions={0}, use_global_device_ids=true | all-gather | bytes 2304 | tf_op jit(solution)/shard_map/all_gather | solution.py:141
  377.1 15.1 %fusion.73 = f32[640,5248]{1,0:T(8,128)} fusion(bf16[1024,5248]{1,0:T(8,128)(2,1)} %all-gather.13.cloned.1.call-done, f32[640,1024]{1,0:T(8,128)} %copy-done.6, f32[1024]{0:T(1024)S(1)} %bitcast.226, f32[640]{0:T(1024)S(1)} %fusion.67, f32[640]{0:T(1024)S(1)} %broadcast_multiply_fusion.1), kind=kOutput, calls=%fused_computation.125 | convolution fusion | flops 6881280000 | bytes 26813440 | tf_op jit(solution)/shard_map/dot_general | solution.py:168
  404.5 15.2 %add_convert_fusion = (bf16[640,2624]{1,0:T(8,128)(2,1)S(1)}, bf16[640,2624]{1,0:T(8,128)(2,1)}, bf16[640,2624]{1,0:T(8,128)(2,1)}) fusion(f32[640,5248]{1,0:T(8,128)} %fusion.73, bf16[2624,1024]{1,0:T(8,128)(2,1)} %all-gather.15.cloned.1.call-done, bf16[1,640,1024]{2,1,0:T(8,128)(2,1)} %param.13), kind=kOutput, calls=%fused_computation.48 | convolution fusion | flops 3471237120 | bytes 30195712 | tf_op jit(solution)/shard_map/dot_general | solution.py:51
  419.7 14.6 multiply_reduce_fusion.2
  463.4 17.3 %all-to-all-done.2 = bf16[4,2,81920]{2,1,0:T(2,128)(2,1)} async-done(((bf16[4,2,81920]{2,1,0:T(2,128)(2,1)}), bf16[4,2,81920]{2,1,0:T(2,128)(2,1)}, u32[]{:S(2)}, u32[]{:S(2)}) %all-to-all-start.2) | async-done | bytes 1310752 | tf_op jit(solution)/shard_map/all_to_all | solution.py:197
  487.1 322.0 %while.46 = (s32[]{:T(128)}, f32[2560,4,64]{0,2,1:T(8,128)}, f32[2560,4,64]{0,2,1:T(8,128)}, bf16[5,512,4,64]{1,3,2,0:T(8,128)(2,1)}, bf16[5,512,4,64]{1,3,2,0:T...) while((s32[]{:T(128)}, f32[2560,4,64]{0,2,1:T(8,128)}, ...), condition=%wide.region_12.13_spmd.clone, body=%wide.region_10.12_spmd.clone.sunk | while | flops 3421763584 | bytes 173334672 | solution.py:119
  511.7 14.3 multiply_reduce_fusion.8
  526.1 14.3 multiply_convert_fusion.7
  575.5 14.3 multiply_reduce_fusion.8
  589.9 14.3 multiply_convert_fusion.7
  654.4 14.3 multiply_convert_fusion.7
  719.0 14.3 multiply_convert_fusion.7
  829.8 63.3 %all_to_all.54 = bf16[1,2560,3,256]{3,2,0,1:T(4,128)(2,1)S(1)} all-to-all(bf16[1,2560,3,256]{3,2,0,1:T(4,128)(2,1)} %copy.65), channel_id=1, replica_groups=mesh['fsdp'=8,'seq'=4] {'seq'}, dimensions={1} | all-to-all | bytes 7864320 | tf_op jit(solution)/shard_map/all_to_all | solution.py:199
  938.4 15.5 %convolution_convert_fusion = bf16[1024,5248]{1,0:T(8,128)(2,1)} fusion(bf16[640,2624]{1,0:T(8,128)(2,1)} %get-tuple-element.245, bf16[640,2624]{1,0:T(8,128)(2,1)} %copy-done.39, f32[640,1024]{1,0:T(8,128)} %copy-done.6, f32[1024]{0:T(1024)S(1)} %bitcast.229, f32[640]{0:T(1024)S(1)} %copy-done.34, f32[640]{0:T(1024)S(1)} %copy-done.22), kind=kOutput, calls=%fused_computation.44 | convolution fusion | flops 6900088832 | bytes 20096000 | tf_op jit(solution)/shard_map/dot_general | solution.py:45
  953.9 85.7 %reduce-scatter.5.cloned.1.call-done = bf16[128,3072]{1,0:T(8,128)(2,1)} async-done(((bf16[1024,3072]{1,0:T(8,128)(2,1)}), bf16[128,3072]{1,0:T(8,128)(2,1)}) %reduce-scatter.5.cloned.1.call-update) | async-done | bytes 786448 | tf_op jit(solution)/shard_map/reduce_scatter | solution.py:216
  1059.4 50.4 %reduce-scatter.7.cloned.1.call-done = bf16[128,1024]{1,0:T(8,128)(2,1)} async-done(((bf16[1024,1024]{1,0:T(8,128)(2,1)}), bf16[128,1024]{1,0:T(8,128)(2,1)}) %reduce-scatter.7.cloned.1.call-update) | async-done | bytes 262160 | tf_op jit(solution)/shard_map/reduce_scatter | solution.py:219
  1109.8 107.1 %reduce-scatter.11.cloned.1.call-done = bf16[328,1024]{1,0:T(8,128)(2,1)} async-done(((bf16[2624,1024]{1,0:T(8,128)(2,1)}), bf16[328,1024]{1,0:T(8,128)(2,1)}) %reduce-scatter.11.cloned.1.call-update) | async-done | bytes 671760 | tf_op jit(solution)/shard_map/reduce_scatter | solution.py:225
  1217.0 185.4 %reduce-scatter.9.cloned.1.call-done = bf16[128,5248]{1,0:T(8,128)(2,1)} async-done(((bf16[1024,5248]{1,0:T(8,128)(2,1)}), bf16[128,5248]{1,0:T(8,128)(2,1)}) %reduce-scatter.9.cloned.1.call-update) | async-done | bytes 1343504 | tf_op jit(solution)/shard_map/reduce_scatter | solution.py:222
  1405.9 19.5 %all-reduce.4 = (bf16[1024]{0:T(1024)(128)(2,1)S(1)}, bf16[1024]{0:T(1024)(128)(2,1)S(1)}) all-reduce(bf16[1024]{0:T(1024)(128)(2,1)S(1)} %get-tuple-element.199, bf16[1024]{0:T(1024)(128)(2,1)S(1)} %copy-done.35), channel_id=3, replica_groups=mesh['fsdp'=8,'seq'=4] {'fsdp'}, use_global_device_ids=true, to_apply=%region_16.17.clone | all-reduce | flops 2048 | bytes 8192
  1440.4 48.7 %all-reduce.9.cloned.1.call-done = (bf16[128,1024]{1,0:T(8,128)(2,1)}, bf16[128,5248]{1,0:T(8,128)(2,1)}, bf16[328,1024]{1,0:T(8,128)(2,1)}) async-done(((bf16[128,1024]{1,0:T(8,128)(2,1)}, bf16[128,5248]{1,0:T(8,128)(2,1)}, bf16[328,1024]{1,0:T(8,128)(2,1)}), (bf16[128,1024]{1,0:T(8,128)(2,1)}, bf16[128,5248]{1,0:T(8,128)(2,1)}, bf16[328,1024]{1,0:T(8,128)(2,1)})) %all-reduce.9.cloned.1.call-update) | async-done | bytes 2277392 | tf_op jit(solution)/shard_map/psum | solution.py:233
  (258 shorter events, 595.2 us)
Async XLA Ops:
  7.2 104.8 %all-gather.9.cloned.1.call-start = ((), (), s32[]{:S(2)}) async-start(), calls=%async_computation.8 | async-start | bytes 7077888 | tf_op jit(solution)/shard_map/all_gather | solution.py:139
  7.9 363.6 %all-gather.11.cloned.1.call-start = ((), (), s32[]{:S(2)}) async-start(), calls=%async_computation.9 | async-start | bytes 2359296 | tf_op jit(solution)/shard_map/all_gather | solution.py:140
  8.7 368.4 %all-gather.13.cloned.1.call-start = ((), (), s32[]{:S(2)}) async-start(), calls=%async_computation.10 | async-start | bytes 12091392 | tf_op jit(solution)/shard_map/all_gather | solution.py:142
  31.9 88.7 %copy-start.25 = (f32[8,1,128]{2,1,0:T(1,128)}, f32[8,1,128]{2,1,0:T(1,128)S(1)}, u32[]{:S(2)}) copy-start(f32[8,1,128]{2,1,0:T(1,128)S(1)} %convert_element_type.215) | copy-start | bytes 12292
  32.3 98.8 %copy-start.13 = (f32[640,64]{0,1:T(8,128)}, f32[640,64]{0,1:T(8,128)S(1)}, u32[]{:S(2)}) copy-start(f32[640,64]{0,1:T(8,128)S(1)} %get-tuple-element.254) | copy-start | bytes 491524
  32.4 98.8 %copy-start.15 = (f32[640,64]{0,1:T(8,128)}, f32[640,64]{0,1:T(8,128)S(1)}, u32[]{:S(2)}) copy-start(f32[640,64]{0,1:T(8,128)S(1)} %get-tuple-element.255) | copy-start | bytes 491524
  32.6 88.0 %copy-start.19 = (f32[640]{0:T(1024)}, f32[640]{0:T(1024)S(1)}, u32[]{:S(2)}) copy-start(f32[640]{0:T(1024)S(1)} %broadcast_multiply_fusion.2) | copy-start | bytes 7684
  33.7 86.9 %copy-start.27 = (f32[640]{0:T(1024)}, f32[640]{0:T(1024)S(1)}, u32[]{:S(2)}) copy-start(f32[640]{0:T(1024)S(1)} %fusion.66) | copy-start | bytes 7684
  141.5 64.5 %all-to-all-start = ((bf16[1,640,3,1024]{1,2,0,3:T(4,128)(2,1)}), bf16[1,640,3,1024]{1,2,0,3:T(4,128)(2,1)}, u32[]{:S(2)}, u32[]{:S(2)}) async-start(bf16[1,640,3,1024]{1,2,0,3:T(4,128)(2,1)} %pad_maximum_fusion.1), calls=%async_computation | async-start | bytes 10485760 | tf_op jit(solution)/shard_map/all_to_all | solution.py:161
  146.6 257.9 %all-gather.15.cloned.1.call-start = ((), (), s32[]{:S(2)}) async-start(), calls=%async_computation.11 | async-start | bytes 6045696 | tf_op jit(solution)/shard_map/all_gather | solution.py:143
  344.0 21.2 %all-to-all-start.1 = ((bf16[4,2,81920]{2,1,0:T(2,128)(2,1)}), bf16[4,2,81920]{2,1,0:T(2,128)(2,1)S(1)}, u32[]{:S(2)}, u32[]{:S(2)}) async-start(bf16[4,2,81920]{2,1,0:T(2,128)(2,1)} %reshape.444), calls=%async_computation.1 | async-start | bytes 2621440 | tf_op jit(solution)/shard_map/all_to_all | solution.py:163
  365.2 69.1 %copy-start.31 = (f32[8,1,128]{2,1,0:T(1,128)}, f32[8,1,128]{2,1,0:T(1,128)S(1)}, u32[]{:S(2)}) copy-start(f32[8,1,128]{2,1,0:T(1,128)S(1)} %convert_element_type.216) | copy-start | bytes 12292
  375.2 59.1 %copy-start.21 = (f32[640]{0:T(1024)}, f32[640]{0:T(1024)S(1)}, u32[]{:S(2)}) copy-start(f32[640]{0:T(1024)S(1)} %broadcast_multiply_fusion.1) | copy-start | bytes 7684
  377.0 57.3 %copy-start.33 = (f32[640]{0:T(1024)}, f32[640]{0:T(1024)S(1)}, u32[]{:S(2)}) copy-start(f32[640]{0:T(1024)S(1)} %fusion.67) | copy-start | bytes 7684
  459.0 21.6 %all-to-all-start.2 = ((bf16[4,2,81920]{2,1,0:T(2,128)(2,1)}), bf16[4,2,81920]{2,1,0:T(2,128)(2,1)}, u32[]{:S(2)}, u32[]{:S(2)}) async-start(bf16[4,2,81920]{2,1,0:T(2,128)(2,1)} %reshape.446), calls=%async_computation.2 | async-start | bytes 2621440 | tf_op jit(solution)/shard_map/all_to_all | solution.py:197
  463.3 576.3 %reduce-scatter.5.cloned.1.call-start = ((), (), s32[]{:S(2)}) async-start(), calls=%async_computation.12 | async-start | bytes 7077888 | tf_op jit(solution)/shard_map/reduce_scatter | solution.py:216
  924.2 185.6 %reduce-scatter.7.cloned.1.call-start = ((), (), s32[]{:S(2)}) async-start(), calls=%async_computation.13 | async-start | bytes 2359296 | tf_op jit(solution)/shard_map/reduce_scatter | solution.py:219
  929.2 287.8 %reduce-scatter.11.cloned.1.call-start = ((), (), s32[]{:S(2)}) async-start(), calls=%async_computation.15 | async-start | bytes 6045696 | tf_op jit(solution)/shard_map/reduce_scatter | solution.py:225
  937.7 464.7 %reduce-scatter.9.cloned.1.call-start = ((), (), s32[]{:S(2)}) async-start(), calls=%async_computation.14 | async-start | bytes 12091392 | tf_op jit(solution)/shard_map/reduce_scatter | solution.py:222
  953.8 86.1 %copy-start.38 = (u32[32]{0:T(128)S(1)}, u32[32]{0:T(128)}, u32[]{:S(2)}) copy-start(u32[32]{0:T(128)} %constant.111) | copy-start | bytes 388
  953.8 482.7 %all-gather.17.cloned.1.call-start = ((), (), s32[]{:S(2)}) async-start(), calls=%async_computation.16 | async-start | bytes 3932160 | tf_op jit(solution)/shard_map/all_gather | solution.py:232
  1039.6 449.5 %all-reduce.9.cloned.1.call-start = ((), (), s32[]{:S(2)}) async-start(), calls=%async_computation.17 | async-start | bytes 4554752 | tf_op jit(solution)/shard_map/psum | solution.py:233
  1402.4 30.2 %copy-start.2 = (f32[640,1024]{1,0:T(8,128)S(1)}, f32[640,1024]{1,0:T(8,128)}, u32[]{:S(2)}) copy-start(f32[640,1024]{1,0:T(8,128)} %copy-done.1) | copy-start | bytes 7864324
  1402.4 30.2 %copy-start.30 = (f32[640]{0:T(1024)S(1)}, f32[640]{0:T(1024)}, u32[]{:S(2)}) copy-start(f32[640]{0:T(1024)} %copy-done.29) | copy-start | bytes 7684
  (31 other events, 154.8 us)
Sparse Core Ops, SparseCore 0:
  10.2 101.7 all-gather.8
  114.1 47.4 all-gather.10
  163.8 152.5 all-gather.12
  318.4 86.0 all-gather.14
  924.3 115.2 reduce-scatter.4
  1043.0 66.7 reduce-scatter.6
  1113.4 103.4 reduce-scatter.10
  1221.0 181.3 reduce-scatter.8
  1404.0 27.7 all-gather.16
  1434.2 54.9 all-reduce.8
